TPU v7x, 32 devices: a whole 2x2x4 slice. The times are simulated.
32 devices in a mesh: groups: 2 (over y), seq: 4 (over z), head: 2 (over x), cfg: 2 (over core).
Axes of the slice: x: 2, y: 2, z: 4, core: 2. Of those that a mesh axis runs over, the one named last changes fastest.
Arguments:
- queries: bfloat16 [2, 1024, 3072], P('cfg', ('groups', 'seq'), 'head'), parts along dimension 1, may hold values from -60 to 60
- keys: bfloat16 [2, 1024, 3072], P('cfg', ('groups', 'seq'), 'head'), parts along dimension 1, may hold values from -3 to 3
- values: bfloat16 [2, 1024, 3072], P('cfg', ('groups', 'seq'), 'head'), parts along dimension 1, may hold values from -6 to 6
- band_mask: int32 [48, 4, 4], P(('groups', 'head')), parts along dimension 0, may hold values from 0 to 1, as said below
- out_weight: bfloat16 [3072, 3072], P('head', 'cfg'), may hold values from -0.109375 to 0.109375
- guidance: float32 [1], replicated, may hold values from 3 to 8
Outputs:
- projected: bfloat16 [1024, 3072], P(('groups', 'seq'), ('cfg', 'head')), parts along dimension 0
There are 2 independent parts, one for each index of `groups`. A program takes and returns all parts, laid end to end along the dimension named above; an argument that names none is the same for every part. Nothing has to cross between parts.
Inputs may be any that keep to these rules, and one draw needn't show every extreme that they name: `band_mask`: densities are drawn per head.
All inputs are finite; a program needn't handle non-finite values.
Results may differ from a plain program's by a relative error of at most 0.02.
Values may be sent and summed in bfloat16 or wider, within the bound.
A program may use at most 128 MiB of HBM per device.

v0:
```python
import jax
import jax.numpy as jnp
from jax import lax
from jax.sharding import PartitionSpec as P

HD = 128


def swapped(array, axis, bit):
    return lax.ppermute(array, axis, [(i, i ^ 1 << bit) for i in range(lax.axis_size(axis))])


def shards(queries, keys, values, band_mask, out_weight, guidance):
    own_q = queries[0]
    own_k = keys[0]
    own_v = values[0]
    q_rows = own_q.shape[0]
    kv_rows = own_k.shape[0]
    local_heads = own_q.shape[1] // HD
    tiles = lax.axis_size("seq")
    place = lax.axis_index("seq")
    scale = HD ** (-0.5)
    bands = jnp.arange(tiles)
    ident = (bands[:, None] == bands[None, :]).astype(jnp.int32)
    allowed = band_mask + ident[None] > 0
    q_heads = own_q.reshape(q_rows, local_heads, HD)
    my_row = lax.dynamic_index_in_dim(allowed, place, 1, keepdims=False)
    k_piece = lax.all_gather(own_k, "seq", axis=0, tiled=True)
    v_piece = lax.all_gather(own_v, "seq", axis=0, tiled=True)
    count = k_piece.shape[0]
    band = jnp.arange(count) // kv_rows
    onehot = band[:, None] == bands[None, :]
    keymask = jnp.any(onehot[None] & my_row[:, None, :], axis=-1)
    top = jnp.full((local_heads, q_rows), -1e30, jnp.float32)
    k_heads = k_piece.reshape(count, local_heads, HD)
    v_heads = v_piece.reshape(count, local_heads, HD)
    scores = (
        jnp.einsum("qhd,khd->hqk", q_heads, k_heads, preferred_element_type=jnp.float32) * scale
    )
    scores = jnp.where(keymask[:, None, :], scores, -1e30)
    new_top = jnp.maximum(top, jnp.max(scores, axis=-1))
    expo = jnp.where(keymask[:, None, :], jnp.exp(scores - new_top[..., None]), 0.0)
    total = jnp.sum(expo, axis=-1)
    accum = jnp.einsum(
        "hqk,khd->hqd", expo.astype(jnp.bfloat16), v_heads, preferred_element_type=jnp.float32
    )
    top, total, accum = (new_top, total, accum)
    attn = accum / total[..., None]
    own_rows = jnp.transpose(attn, (1, 0, 2)).reshape(q_rows, local_heads * HD).astype(jnp.bfloat16)
    partner = swapped(own_rows, "cfg", 0)
    first_copy = lax.axis_index("cfg") == 0
    cond = jnp.where(first_copy, own_rows, partner).astype(jnp.float32)
    uncond = jnp.where(first_copy, partner, own_rows).astype(jnp.float32)
    guided = (uncond + guidance[0] * (cond - uncond)).astype(jnp.bfloat16)
    terms = jnp.dot(guided, out_weight, preferred_element_type=jnp.float32)
    return lax.psum_scatter(terms.astype(jnp.bfloat16), "head", scatter_dimension=1, tiled=True)


def solution(mesh):
    in_specs = (
        P("cfg", ("groups", "seq"), "head"),
        P("cfg", ("groups", "seq"), "head"),
        P("cfg", ("groups", "seq"), "head"),
        P(("groups", "head"), None, None),
        P("head", "cfg"),
        P(),
    )
    out_specs = P(("groups", "seq"), ("cfg", "head"))
    return jax.shard_map(shards, mesh=mesh, in_specs=in_specs, out_specs=out_specs, check_vma=False)
```

profile of v0, /device:TPU:0, one launch (start us, length us, event | category | flops | bytes accessed | tf_op | source)
XLA Modules:
  0.0 115.7 jit_solution(17461585019683338702)
XLA Ops:
  6.5 0.0 all-gather.5.cloned.1.call-start
  6.5 1.9 %copy.18 = bf16[1,128,1536]{1,2,0:T(8,128)(2,1)} copy(bf16[1,128,1536]{2,1,0:T(8,128)(2,1)} %param.7) | data formatting | bytes 786432 | tf_op args[1]
  8.4 0.0 all-gather.5.cloned.1.call-update
  8.5 0.0 all-gather.7.cloned.1.call-start
  8.5 0.7 all-gather.7.cloned.1.call-update
  9.2 0.0 reduce-scatter.2.cloned.1.call-start
  9.3 0.8 fusion.31
  10.1 0.1 copy.16
  10.2 1.2 %copy.17 = bf16[1,128,1536]{1,2,0:T(8,128)(2,1)S(1)} copy(bf16[1,128,1536]{2,1,0:T(8,128)(2,1)} %param.6) | data formatting | bytes 786432 | tf_op args[0]
  11.4 0.1 and_reduce_fusion
  11.6 37.8 %all-gather.5.cloned.1.call-done = bf16[1,512,1536]{1,2,0:T(8,128)(2,1)} async-done(((bf16[1,128,1536]{1,2,0:T(8,128)(2,1)}), bf16[1,512,1536]{1,2,0:T(8,128)(2,1)}) %all-gather.5.cloned.1.call-update) | async-done | bytes 1572880 | tf_op jit(solution)/shard_map/all_gather | solution.py:28
  49.3 2.2 %fusion = (f32[12,128]{1,0:T(8,128)S(1)}, f32[12,128,512]{2,1,0:T(8,128)S(1)}) fusion(pred[12,512]{1,0:T(8,128)(4,1)S(1)} %and_reduce_fusion, bf16[128,12,128]{0,2,1:T(8,128)(2,1)S(1)} %bitcast.20, bf16[512,12,128]{0,2,1:T(8,128)(2,1)} %bitcast.21), kind=kOutput, calls=%fused_computation.2 | convolution fusion | flops 203684352 | bytes 5124096 | tf_op jit(solution)/shard_map/qhd,khd->hqk/dot_general | solution.py:38
  51.5 1.6 %fusion.1 = f32[12,128]{1,0:T(8,128)} fusion(f32[12,128,512]{2,1,0:T(8,128)S(1)} %get-tuple-element.6, f32[12,128]{1,0:T(8,128)S(1)} %broadcast_maximum_fusion, pred[12,512]{1,0:T(8,128)(4,1)S(1)} %and_reduce_fusion), kind=kLoop, calls=%fused_computation.4 | loop fusion | flops 3930624 | bytes 3164160 | tf_op jit(solution)/shard_map/reduce_sum | solution.py:43
  53.1 33.1 %all-gather.7.cloned.1.call-done = bf16[1,512,1536]{2,1,0:T(8,128)(2,1)} async-done(((bf16[1,128,1536]{2,1,0:T(8,128)(2,1)}), bf16[1,512,1536]{2,1,0:T(8,128)(2,1)}) %all-gather.7.cloned.1.call-update) | async-done | bytes 1572880 | tf_op jit(solution)/shard_map/all_gather | solution.py:29
  86.2 2.6 %copy.21 = bf16[1,512,1536]{1,2,0:T(8,128)(2,1)} copy(bf16[1,512,1536]{2,1,0:T(8,128)(2,1)} %all-gather.7.cloned.1.call-done) | data formatting | bytes 3145728 | tf_op jit(solution)/shard_map/all_gather | solution.py:29
  88.8 2.4 %fusion.16 = bf16[128,12,128]{0,2,1:T(8,128)(2,1)S(1)} fusion(bf16[512,12,128]{0,2,1:T(8,128)(2,1)} %bitcast.19, f32[12,128,512]{2,1,0:T(8,128)S(1)} %get-tuple-element.6, f32[12,128]{1,0:T(8,128)S(1)} %broadcast_maximum_fusion, pred[12,512]{1,0:T(8,128)(4,1)S(1)} %and_reduce_fusion, f32[128,12]{0,1:T(8,128)} %bitcast.24), kind=kOutput, calls=%fused_computation.16 | convolution fusion | flops 205651968 | bytes 5130240 | tf_op jit(solution)/shard_map/hqk,khd->hqd/dot_general | solution.py:44
  91.2 0.1 collective-permute-start
  91.9 1.1 collective-permute-done
  93.0 3.9 %convolution_convert_fusion = bf16[128,1536]{1,0:T(8,128)(2,1)} fusion(bf16[1536,1536]{1,0:T(8,128)(2,1)} %param.10, bf16[128,1536]{0,1:T(8,128)(2,1)S(1)} %bitcast.23, bf16[128,1536]{0,1:T(8,128)(2,1)S(1)} %collective-permute-done, f32[]{:T(128)} %bitcast.18, pred[]{:T(512)S(6)} %eq.37), kind=kOutput, calls=%fused_computation.3 | convolution fusion | flops 605749248 | bytes 5898245 | tf_op jit(solution)/shard_map/dot_general | solution.py:55
  96.9 0.0 reduce-scatter.2.cloned.1.call-update
  96.9 12.2 %reduce-scatter.2.cloned.1.call-done = bf16[128,768]{1,0:T(8,128)(2,1)} async-done(((bf16[128,1536]{1,0:T(8,128)(2,1)}), bf16[128,768]{1,0:T(8,128)(2,1)}) %reduce-scatter.2.cloned.1.call-update) | async-done | bytes 196624 | tf_op jit(solution)/shard_map/reduce_scatter | solution.py:56
  (5 shorter events, 0.0 us)
Async XLA Ops:
  6.5 42.8 %all-gather.5.cloned.1.call-start = ((), (), s32[]{:S(2)}) async-start(), calls=%async_computation.2 | async-start | bytes 1966080 | tf_op jit(solution)/shard_map/all_gather | solution.py:28
  8.5 77.7 %all-gather.7.cloned.1.call-start = ((), (), s32[]{:S(2)}) async-start(), calls=%async_computation.3 | async-start | bytes 1966080 | tf_op jit(solution)/shard_map/all_gather | solution.py:29
  9.2 99.9 %reduce-scatter.2.cloned.1.call-start = ((), (), s32[]{:S(2)}) async-start(), calls=%async_computation.1 | async-start | bytes 589824 | tf_op jit(solution)/shard_map/reduce_scatter | solution.py:56
  91.2 1.8 %collective-permute-start = (bf16[128,1536]{0,1:T(8,128)(2,1)S(1)}, bf16[128,1536]{0,1:T(8,128)(2,1)S(1)}, u32[]{:S(2)}, u32[]{:S(2)}) collective-permute-start(bf16[128,1536]{0,1:T(8,128)(2,1)S(1)} %bitcast.22), channel_id=1, source_target_pairs={{0,1},{1,0},{2,3},{3,2},{4,5},{5,4},{6,7},{7,6},{8,9},{9,8},{10,11... | collective-permute-start | bytes 1179656 | tf_op jit(solution)/shard_map/ppermute | solution.py:10
Sparse Core Ops, SparseCore 0:
  8.9 40.3 all-gather.4
  50.9 35.2 all-gather.6
  97.0 12.0 reduce-scatter.1
where the time goes:
time: 116 us
  waiting for transfers between devices  84.8 us (73%)
  between operations  13.8 us (12%)
  matrix products  8.47 us (7%)
  local copies, waits for them, and re-layouts  5.84 us (5%)
  other arithmetic  2.52 us (2%)
    all_gather x1, waiting for transfers between devices, shards(): k_piece = lax.all_gather(own_k, 'seq', axis=0, tiled=True)  37.8 us
    all_gather x1, waiting for transfers between devices, shards(): v_piece = lax.all_gather(own_v, 'seq', axis=0, tiled=True)  33.1 us
    reduce_scatter x1, waiting for transfers between devices, shards(): lax.psum_scatter(terms.astype(jnp.bfloat16), 'head', scatter_dimension=1,...  12.2 us
    dot_general x1, matrix products, shards(): terms = jnp.dot(guided, out_weight, preferred_element_type=jnp.float32)  3.91 us
    unnamed x2, local copies, waits for them, and re-layouts  3.12 us
    all_gather x1, local copies, waits for them, and re-layouts, shards(): v_piece = lax.all_gather(own_v, 'seq', axis=0, tiled=True)  2.6 us
    dot_general x1, matrix products, shards(): jnp.einsum('hqk,khd->hqd', expo.astype(jnp.bfloat16), v_heads, preferred_...  2.39 us
  transfers between devices with their start and end apart: 4, of which 4 were waited for; matrix products, arithmetic and copies ran while one was open for 5% of the time, Pallas kernels for 0%

commit v1 on v0

--- a/solution.py
+++ b/solution.py
@@ -1,16 +1,233 @@
+import functools
+
 import jax
 import jax.numpy as jnp
 from jax import lax
+from jax.experimental import pallas as pl
+from jax.experimental.pallas import tpu as pltpu
 from jax.sharding import PartitionSpec as P
 
 HD = 128
+MESH = pl.DeviceIdType.MESH
+LOG2E = 1.4426950408889634
+
+
+def flipped(index, bits):
+    out = index
+    bit = 1
+    while bit <= bits:
+        if bits // bit % 2:
+            out = out + bit - 2 * bit * lax.rem(lax.div(index, bit), 2)
+        bit *= 2
+    return out
+
+
+def remote(src, dst, send, recv, device):
+    copy = pltpu.make_async_remote_copy(
+        src_ref=src, dst_ref=dst, send_sem=send, recv_sem=recv, device_id=device, device_id_type=MESH
+    )
+    copy.start()
+    return copy
+
+
+def kernel(
+    n, hp, parts,
+    q_ref, k_ref, v_ref, mask_ref, w_ref, g_ref, out_ref,
+    q_buf, k_buf, v_buf, w_buf, att, other, guid, rows, acc, sends, recvs,
+    load_sem, w_sem, a_send, a_recv, x_send, x_recv, r_send, r_recv, s_send, s_recv, h_send, h_recv,
+):
+    me = lax.axis_index("seq")
+    core = lax.axis_index("cfg")
+    side = lax.axis_index("head")
+    T = q_ref.shape[1]
+    half = T // 2
+    cols = out_ref.shape[1]
+    width = cols // len(range(0, cols, 256)) if cols % 256 == 0 else cols
+
+    loads = []
+    mine = pl.multiple_of(me * T, T)
+    for i, (ref, buf) in enumerate(((q_ref, q_buf), (k_ref, k_buf), (v_ref, v_buf))):
+        for j in range(hp):
+            at = pl.multiple_of((me * hp + j) * HD, HD)
+            c = pltpu.make_async_copy(ref.at[0, :, pl.ds(at, HD)], buf.at[j, pl.ds(mine, T), :], load_sem.at[j, i])
+            c.start()
+            loads.append(c)
+    sibling = {"cfg": 1 - core}
+    barrier = pltpu.get_barrier_semaphore()
+    for k in range(1, n):
+        pl.semaphore_signal(barrier, inc=1, device_id={"seq": flipped(me, k)}, device_id_type=MESH)
+    pl.semaphore_signal(barrier, inc=1, device_id=sibling, device_id_type=MESH)
+    for d in range(1, parts):
+        pl.semaphore_signal(barrier, inc=1, device_id={"head": lax.rem(side + d, parts)}, device_id_type=MESH)
+    pl.semaphore_wait(barrier, n - 1 + 1 + parts - 1)
+
+    a2a = {}
+    for j in range(hp):
+        for k in range(n - 1, 0, -1):
+            dest = flipped(me, k)
+            at = pl.multiple_of((dest * hp + j) * HD, HD)
+            for i, (ref, buf) in enumerate(((q_ref, q_buf), (k_ref, k_buf), (v_ref, v_buf))):
+                a2a[j, k, i] = remote(
+                    ref.at[0, :, pl.ds(at, HD)], buf.at[j, pl.ds(mine, T), :],
+                    a_send.at[j, k - 1, i], a_recv.at[j, k - 1, i], {"seq": dest},
+                )
+    w_loads = []
+    for j in range(hp):
+        for z in range(n):
+            c = pltpu.make_async_copy(
+                w_ref.at[pl.ds((z * hp + j) * HD, HD), :], w_buf.at[j, pl.ds(z * HD, HD), :], w_sem.at[j, z]
+            )
+            c.start()
+            w_loads.append(c)
+
+    scale = HD ** (-0.5) * LOG2E
+    guidance = g_ref[0]
+    first = core == 0
+    half_at = pl.multiple_of(core * half, half)
+    pending = []
+    backs = {}
+
+    own_at = pl.multiple_of(me * HD, HD)
+    siblings = {}
+    for j in range(hp):
+        for i in range(3):
+            loads[i * hp + j].wait()
+            for k in range(1, n):
+                a2a[j, k, i].wait_recv()
+        head = me * hp + j
+        for t in range(n):
+            q = q_buf[j, t * T:(t + 1) * T, :]
+            s = lax.dot_general(q, k_buf[j], (((1,), (1,)), ((), ())), preferred_element_type=jnp.float32)
+            pieces = []
+            for b in range(n):
+                listed = mask_ref[head, t, b] > 0
+                bias = 0.0 if b == t else jnp.where(listed, 0.0, -1e30).astype(jnp.float32)
+                pieces.append(s[:, b * T:(b + 1) * T] * scale + bias)
+            s = jnp.concatenate(pieces, axis=1)
+            top = jnp.max(s, axis=1, keepdims=True)
+            expo = jnp.exp2(s - top)
+            total = jnp.sum(expo, axis=1, keepdims=True)
+            o = jnp.dot(expo.astype(jnp.bfloat16), v_buf[j], preferred_element_type=jnp.float32)
+            o = (o * (1.0 / total)).astype(jnp.bfloat16)
+            att[j, 0, t] = o[:half]
+            att[j, 1, t] = o[half:]
+        swap = remote(att.at[j, 1 - core], other.at[j], x_send.at[j], x_recv.at[j], sibling)
+        swap.wait_recv()
+        own = att[j, core].astype(jnp.float32)
+        oth = other[j].astype(jnp.float32)
+        cond = jnp.where(first, own, oth)
+        uncond = jnp.where(first, oth, own)
+        guid[j] = (uncond + guidance * (cond - uncond)).astype(jnp.bfloat16)
+        for k in range(n - 1, 0, -1):
+            dest = flipped(me, k)
+            backs[j, k] = remote(
+                guid.at[j, dest], rows.at[j, pl.ds(half_at, half), pl.ds(own_at, HD)],
+                r_send.at[j, k - 1], r_recv.at[j, k - 1], {"seq": dest},
+            )
+        siblings[j] = [remote(
+            guid.at[j, me], rows.at[j, pl.ds(half_at, half), pl.ds(own_at, HD)], s_send.at[j, 0], s_recv.at[j, 0], sibling
+        )]
+        rows[j, pl.ds(half_at, half), pl.ds(own_at, HD)] = guid[j, me]
+        pending.append(swap)
+
+        def forward(j):
+            for k in range(1, n):
+                backs[j, k].wait_recv()
+                at = pl.multiple_of(flipped(me, k) * HD, HD)
+                block = rows.at[j, pl.ds(half_at, half), pl.ds(at, HD)]
+                siblings[j].append(remote(block, block, s_send.at[j, k], s_recv.at[j, k], sibling))
+
+        if j > 0:
+            forward(j - 1)
+    forward(hp - 1)
+
+    for c in w_loads:
+        c.wait()
+    for j in range(hp - 1):
+        for copy in siblings[j]:
+            copy.wait_recv()
+        term = jnp.dot(rows[j], w_buf[j], preferred_element_type=jnp.float32)
+        acc[...] = term if j == 0 else acc[...] + term
+    j = hp - 1
+    for copy in siblings[j]:
+        copy.wait_recv()
+    last = rows[j]
+    outs = []
+    for d in range(1, parts + 1):
+        to = lax.rem(side + d, parts)
+        for p in range(cols // width):
+            at = pl.multiple_of(to * cols + p * width, width)
+            term = jnp.dot(last, w_buf[j, :, pl.ds(at, width)], preferred_element_type=jnp.float32)
+            if hp > 1:
+                term = term + acc[:, pl.ds(at, width)]
+            span = pl.ds(p * width, width)
+            if d < parts:
+                sends[d - 1, p] = term.astype(jnp.bfloat16)
+                outs.append(remote(
+                    sends.at[d - 1, p], recvs.at[d - 1, p], h_send.at[d - 1, p], h_recv.at[d - 1, p], {"head": to}
+                ))
+            else:
+                acc[:, pl.ds(at, width)] = term
+    for p in range(cols // width):
+        at = pl.multiple_of(side * cols + p * width, width)
+        total = acc[:, pl.ds(at, width)]
+        for d in range(1, parts):
+            outs[(d - 1) * (cols // width) + p].wait_recv()
+            total = total + recvs[d - 1, p].astype(jnp.float32)
+        out_ref[:, p * width:(p + 1) * width] = total.astype(jnp.bfloat16)
+    for copy in list(a2a.values()) + pending + list(backs.values()) + sum(siblings.values(), []) + outs:
+        copy.wait_send()
+
+
+def by_heads(queries, keys, values, band_mask, out_weight, guidance):
+    n = lax.axis_size("seq")
+    parts = lax.axis_size("head")
+    T, local = queries.shape[1], queries.shape[2]
+    hp = local // HD // n
+    wide = out_weight.shape[1]
+    cols = wide // parts
+    width = 256 if cols % 256 == 0 else cols
+    half = T // 2
+    bf, f32 = jnp.bfloat16, jnp.float32
+    any_spec = pl.BlockSpec(memory_space=pl.ANY)
+    smem = pl.BlockSpec(memory_space=pltpu.SMEM)
+    dma = pltpu.SemaphoreType.DMA
+    return pl.pallas_call(
+        functools.partial(kernel, n, hp, parts),
+        out_shape=jax.ShapeDtypeStruct((T, cols), bf),
+        in_specs=[any_spec, any_spec, any_spec, smem, any_spec, smem],
+        out_specs=pl.BlockSpec(memory_space=pltpu.VMEM),
+        scratch_shapes=[
+            pltpu.VMEM((hp, n * T, HD), bf),
+            pltpu.VMEM((hp, n * T, HD), bf),
+            pltpu.VMEM((hp, n * T, HD), bf),
+            pltpu.VMEM((hp, n * HD, wide), bf),
+            pltpu.VMEM((hp, 2, n, half, HD), bf),
+            pltpu.VMEM((hp, n, half, HD), bf),
+            pltpu.VMEM((hp, n, half, HD), bf),
+            pltpu.VMEM((hp, T, n * HD), bf),
+            pltpu.VMEM((T, wide), f32),
+            pltpu.VMEM((parts - 1, cols // width, T, width), bf),
+            pltpu.VMEM((parts - 1, cols // width, T, width), bf),
+            dma((hp, 3)), dma((hp, n)),
+            dma((hp, n - 1, 3)), dma((hp, n - 1, 3)),
+            dma((hp,)), dma((hp,)),
+            dma((hp, n - 1)), dma((hp, n - 1)),
+            dma((hp, n)), dma((hp, n)),
+            dma((parts - 1, cols // width)), dma((parts - 1, cols // width)),
+        ],
+        compiler_params=pltpu.CompilerParams(
+            collective_id=0, has_side_effects=True, vmem_limit_bytes=60 * 1024 * 1024
+        ),
+        name="by_heads",
+    )(queries, keys, values, band_mask, out_weight, guidance)
 
 
 def swapped(array, axis, bit):
     return lax.ppermute(array, axis, [(i, i ^ 1 << bit) for i in range(lax.axis_size(axis))])
 
 
-def shards(queries, keys, values, band_mask, out_weight, guidance):
+def by_rows(queries, keys, values, band_mask, out_weight, guidance):
     own_q = queries[0]
     own_k = keys[0]
     own_v = values[0]
@@ -56,6 +273,14 @@
     return lax.psum_scatter(terms.astype(jnp.bfloat16), "head", scatter_dimension=1, tiled=True)
 
 
+def shards(queries, *rest):
+    seq = lax.axis_size("seq")
+    heads = queries.shape[2] // HD
+    if heads % seq == 0 and seq & (seq - 1) == 0 and lax.axis_size("cfg") == 2:
+        return by_heads(queries, *rest)
+    return by_rows(queries, *rest)
+
+
 def solution(mesh):
     in_specs = (
         P("cfg", ("groups", "seq"), "head"),

time: 116 us -> 54.3 us (0.47)
  waiting for transfers between devices: 84.8 us -> 0 us
  Pallas kernels: 0 us -> 50.3 us
  between operations: 13.8 us -> 0.66 us
  matrix products: 8.47 us -> 0 us
  local copies, waits for them, and re-layouts: 5.84 us -> 3.02 us
  other arithmetic: 2.52 us -> 0 us
    all_gather x2 -> x0, waiting for transfers between devices: 70.8 us -> none  [the longest x1 37.8 us: shards(): k_piece = lax.all_gather(own_k, 'seq', axis=0, tiled=True)]
    pallas_call x0 -> x1, Pallas kernels: none -> 50.3 us  [by_heads(): pl.pallas_call(functools.partial(kernel, n, hp, parts), out_shape=jax.Sha...]
    reduce_scatter x1 -> x0, waiting for transfers between devices: 12.2 us -> none  [shards(): lax.psum_scatter(terms.astype(jnp.bfloat16), 'head', scatter_dimension=1,...]
    dot_general x3 -> x0, matrix products: 8.47 us -> none  [the longest x1 3.91 us: shards(): terms = jnp.dot(guided, out_weight, preferred_element_type=jnp.float32)]
    all_gather x1 -> x0, local copies, waits for them, and re-layouts: 2.6 us -> none  [shards(): v_piece = lax.all_gather(own_v, 'seq', axis=0, tiled=True)]
    reduce_sum x1 -> x0, other arithmetic: 1.6 us -> none  [shards(): total = jnp.sum(expo, axis=-1)]
  transfers between devices with their start and end apart: 4 -> 0, of which waited for: 4 -> 0; matrix products, arithmetic and copies ran while one was open for 5% -> 0% of each run, Pallas kernels for 0% -> 0%
where the time goes in v1:
time: 54.3 us; the launch traced here: 54 us
  Pallas kernels  50.3 us (93%)
  local copies, waits for them, and re-layouts  3.02 us (6%)
  between operations  0.66 us (1%)
    pallas_call x1, Pallas kernels, by_heads(): pl.pallas_call(functools.partial(kernel, n, hp, parts), out_shape=jax.Sha...  50.3 us
    unnamed x2, local copies, waits for them, and re-layouts  3.02 us

profile of v1, /device:TPU:0, one launch (start us, length us, event | category | flops | bytes accessed | tf_op | source)
XLA Modules:
  0.0 54.0 jit_solution(9524406503895756908)
XLA Ops:
  0.7 1.4 %copy.7.mask_ref = s32[12,4,4]{2,1,0:T(4,128)} copy(s32[12,4,4]{0,2,1:T(4,128)} %param.9) | data formatting | bytes 1536 | tf_op args[3]
  2.1 50.3 %by_heads.1 = bf16[128,768]{1,0:T(8,128)(2,1)} custom-call(bf16[1,128,1536]{2,1,0:T(8,128)(2,1)} %q_ref.1, bf16[1,128,1536]{2,1,0:T(8,128)(2,1)} %k_ref.1, bf16[1,128,1536]{2,1,0:T(8,128)(2,1)} %v_ref.1, s32[12,4,4]{2,1,0:T(4,128)} %copy.7.mask_ref, bf16[1536,1536]{1,0:T(8,128)(2,1)} %w_ref.1, f32[1]{0:T(128)S(6)} %copy.9.g_ref), custom_call_target="tpu_custom_call" | custom-call | tf_op jit(solution)/shard_map/by_heads/pallas_call | solution.py:195
  52.4 1.6 %copy.10 = bf16[128,768]{1,0:T(8,128)(2,1)} copy(bf16[128,768]{1,0:T(8,128)(2,1)} %by_heads.1) | data formatting | bytes 393216

commit v2 on v1

v2 whole, which is shorter than its diff:
```python
import functools

import jax
import jax.numpy as jnp
from jax import lax
from jax.experimental import pallas as pl
from jax.experimental.pallas import tpu as pltpu
from jax.sharding import PartitionSpec as P

HD = 128
MESH = pl.DeviceIdType.MESH
LOG2E = 1.4426950408889634


def flipped(index, bits):
    out = index
    bit = 1
    while bit <= bits:
        if bits // bit % 2:
            out = out + bit - 2 * bit * lax.rem(lax.div(index, bit), 2)
        bit *= 2
    return out


def remote(src, dst, send, recv, device):
    copy = pltpu.make_async_remote_copy(
        src_ref=src, dst_ref=dst, send_sem=send, recv_sem=recv, device_id=device, device_id_type=MESH
    )
    copy.start()
    return copy


def kernel(
    n, hp, sets,
    q_ref, k_ref, v_ref, mask_ref, w_ref, g_ref, out_ref,
    q_buf, k_buf, v_buf, w_buf, att, other, guid, rows, acc,
    load_sem, w_sem, a_send, a_recv, x_send, x_recv, r_send, r_recv, f_send, f_recv,
    wx_send, wx_recv, wy_send, wy_recv,
):
    me = lax.axis_index("seq")
    core = lax.axis_index("cfg")
    side = lax.axis_index("head")
    group = lax.axis_index("groups")
    T = q_ref.shape[1]
    half = T // 2
    cols = out_ref.shape[1]
    share = n // sets
    tensors = ((q_ref, q_buf), (k_ref, k_buf), (v_ref, v_buf))
    sibling = {"cfg": 1 - core}
    across = {"head": 1 - side}
    facing = {"head": 1 - side, "cfg": 1 - core}
    groups = [{"groups": lax.rem(group + d, sets)} for d in range(1, sets)]

    barrier = pltpu.get_barrier_semaphore()
    for device in [{"seq": flipped(me, k)} for k in range(1, n)] + [sibling, across, facing] + groups:
        pl.semaphore_signal(barrier, inc=1, device_id=device, device_id_type=MESH)

    loads = {}
    mine = pl.multiple_of(me * T, T)
    for j in range(hp):
        at = pl.multiple_of((me * hp + j) * HD, HD)
        for i, (ref, buf) in enumerate(tensors):
            loads[j, i] = pltpu.make_async_copy(
                ref.at[0, :, pl.ds(at, HD)], buf.at[j, pl.ds(mine, T), :], load_sem.at[j, i]
            )
            loads[j, i].start()
    w_loads = {}
    own_cols = pl.ds(pl.multiple_of(side * cols, cols), cols)
    for j in range(hp):
        for z in range(n):
            w_loads[j, z] = pltpu.make_async_copy(
                w_ref.at[pl.ds((z * hp + j) * HD, HD), own_cols], w_buf.at[0, j, pl.ds(z * HD, HD), :], w_sem.at[j, z]
            )
    pl.semaphore_wait(barrier, n - 1 + 3 + sets - 1)

    a2a = {}
    across_w = {}
    their_cols = pl.ds(pl.multiple_of((1 - side) * cols, cols), cols)
    for j in range(hp):
        for k in range(n - 1, 0, -1):
            dest = flipped(me, k)
            at = pl.multiple_of((dest * hp + j) * HD, HD)
            for i, (ref, buf) in enumerate(tensors):
                a2a[j, k, i] = remote(
                    ref.at[0, :, pl.ds(at, HD)], buf.at[j, pl.ds(mine, T), :],
                    a_send.at[j, k - 1, i], a_recv.at[j, k - 1, i], {"seq": dest},
                )
        for i in range(share):
            z = group * share + i
            at = pl.multiple_of((z * hp + j) * HD, HD)
            across_w[j, i] = remote(
                w_ref.at[pl.ds(at, HD), their_cols],
                w_buf.at[1, j, pl.ds(pl.multiple_of(z * HD, HD), HD), :],
                wx_send.at[j, i], wx_recv.at[j, i], across,
            )
    for copy in w_loads.values():
        copy.start()

    scale = HD ** (-0.5) * LOG2E
    guidance = g_ref[0]
    first = core == 0
    my_half = pl.ds(pl.multiple_of(core * half, half), half)
    swaps, backs, relays, group_w = {}, {}, {}, {}

    def pass_on(j, src, block, z, at):
        for i, (slot, device) in enumerate(((0, sibling), (1, across), (1, facing))):
            relays[j, src, i] = remote(
                block, rows.at[slot, j, my_half, pl.ds(at, HD)], f_send.at[i, j, src], f_recv.at[i, j, src], device
            )

    for j in range(hp):
        for i in range(share):
            across_w[j, i].wait_recv()
            z = group * share + i
            block = w_buf.at[1, j, pl.ds(pl.multiple_of(z * HD, HD), HD), :]
            for d, device in enumerate(groups):
                group_w[d, j, i] = remote(block, block, wy_send.at[d, j, i], wy_recv.at[d, j, i], device)
        for i in range(3):
            loads[j, i].wait()
            for k in range(1, n):
                a2a[j, k, i].wait_recv()
        head = me * hp + j
        for t in range(n):
            q = q_buf[j, t * T:(t + 1) * T, :]
            s = lax.dot_general(q, k_buf[j], (((1,), (1,)), ((), ())), preferred_element_type=jnp.float32)
            pieces = []
            for b in range(n):
                piece = s[:, b * T:(b + 1) * T] * scale
                if b != t:
                    piece = piece + jnp.where(mask_ref[t, b, head] > 0, 0.0, -1e30).astype(jnp.float32)
                pieces.append(piece)
            s = jnp.concatenate(pieces, axis=1)
            top = jnp.max(s, axis=1, keepdims=True)
            expo = jnp.exp2(s - top)
            total = jnp.sum(expo, axis=1, keepdims=True)
            o = jnp.dot(expo.astype(jnp.bfloat16), v_buf[j], preferred_element_type=jnp.float32)
            o = (o * (1.0 / total)).astype(jnp.bfloat16)
            att[j, 0, t] = o[:half]
            att[j, 1, t] = o[half:]
        swaps[j] = remote(att.at[j, 1 - core], other.at[j], x_send.at[j], x_recv.at[j], sibling)
        swaps[j].wait_recv()
        own = att[j, core].astype(jnp.float32)
        oth = other[j].astype(jnp.float32)
        cond = jnp.where(first, own, oth)
        uncond = jnp.where(first, oth, own)
        guid[j] = (uncond + guidance * (cond - uncond)).astype(jnp.bfloat16)
        own_at = pl.multiple_of(me * HD, HD)
        for k in range(n - 1, 0, -1):
            dest = flipped(me, k)
            backs[j, k] = remote(
                guid.at[j, dest], rows.at[0, j, my_half, pl.ds(own_at, HD)],
                r_send.at[j, k - 1], r_recv.at[j, k - 1], {"seq": dest},
            )
        pass_on(j, 0, guid.at[j, me], me, own_at)
        rows[0, j, my_half, pl.ds(own_at, HD)] = guid[j, me]

    for j in range(hp):
        for k in range(1, n):
            backs[j, k].wait_recv()
            z = flipped(me, k)
            at = pl.multiple_of(z * HD, HD)
            pass_on(j, k, rows.at[0, j, my_half, pl.ds(at, HD)], z, at)

    for copy in w_loads.values():
        copy.wait()
    for copy in group_w.values():
        copy.wait_recv()
    for j in range(hp):
        for slot, kinds in ((0, (0,)), (1, (1, 2))):
            for k in range(n):
                for i in kinds:
                    relays[j, k, i].wait_recv()
            term = jnp.dot(rows[slot, j], w_buf[slot, j], preferred_element_type=jnp.float32)
            if j + slot > 0:
                term = acc[...] + term
            if slot == 1 and j == hp - 1:
                out_ref[...] = term.astype(jnp.bfloat16)
            else:
                acc[...] = term
    for copies in (a2a, across_w, swaps, backs, relays, group_w):
        for copy in copies.values():
            copy.wait_send()


def by_heads(queries, keys, values, band_mask, out_weight, guidance):
    n = lax.axis_size("seq")
    sides = lax.axis_size("head")
    sets = lax.axis_size("groups")
    T, local = queries.shape[1], queries.shape[2]
    hp = local // HD // n
    cols = out_weight.shape[1] // sides
    half = T // 2
    share = n // sets
    bf = jnp.bfloat16
    any_spec = pl.BlockSpec(memory_space=pl.ANY)
    smem = pl.BlockSpec(memory_space=pltpu.SMEM)
    dma = pltpu.SemaphoreType.DMA
    return pl.pallas_call(
        functools.partial(kernel, n, hp, sets),
        out_shape=jax.ShapeDtypeStruct((T, cols), bf),
        in_specs=[any_spec, any_spec, any_spec, smem, any_spec, smem],
        out_specs=pl.BlockSpec(memory_space=pltpu.VMEM),
        scratch_shapes=[
            pltpu.VMEM((hp, n * T, HD), bf),
            pltpu.VMEM((hp, n * T, HD), bf),
            pltpu.VMEM((hp, n * T, HD), bf),
            pltpu.VMEM((sides, hp, n * HD, cols), bf),
            pltpu.VMEM((hp, 2, n, half, HD), bf),
            pltpu.VMEM((hp, n, half, HD), bf),
            pltpu.VMEM((hp, n, half, HD), bf),
            pltpu.VMEM((sides, hp, T, n * HD), bf),
            pltpu.VMEM((T, cols), jnp.float32),
            dma((hp, 3)), dma((hp, n)),
            dma((hp, n - 1, 3)), dma((hp, n - 1, 3)),
            dma((hp,)), dma((hp,)),
            dma((hp, n - 1)), dma((hp, n - 1)),
            dma((3, hp, n)), dma((3, hp, n)),
            dma((hp, share)), dma((hp, share)),
            dma((sets - 1, hp, share)), dma((sets - 1, hp, share)),
        ],
        compiler_params=pltpu.CompilerParams(
            collective_id=0, has_side_effects=True, vmem_limit_bytes=60 * 1024 * 1024
        ),
        name="by_heads",
    )(queries, keys, values, jnp.transpose(band_mask, (1, 2, 0)), out_weight, guidance)


def swapped(array, axis, bit):
    return lax.ppermute(array, axis, [(i, i ^ 1 << bit) for i in range(lax.axis_size(axis))])


def by_rows(queries, keys, values, band_mask, out_weight, guidance):
    own_q = queries[0]
    own_k = keys[0]
    own_v = values[0]
    q_rows = own_q.shape[0]
    kv_rows = own_k.shape[0]
    local_heads = own_q.shape[1] // HD
    tiles = lax.axis_size("seq")
    place = lax.axis_index("seq")
    scale = HD ** (-0.5)
    bands = jnp.arange(tiles)
    ident = (bands[:, None] == bands[None, :]).astype(jnp.int32)
    allowed = band_mask + ident[None] > 0
    q_heads = own_q.reshape(q_rows, local_heads, HD)
    my_row = lax.dynamic_index_in_dim(allowed, place, 1, keepdims=False)
    k_piece = lax.all_gather(own_k, "seq", axis=0, tiled=True)
    v_piece = lax.all_gather(own_v, "seq", axis=0, tiled=True)
    count = k_piece.shape[0]
    band = jnp.arange(count) // kv_rows
    onehot = band[:, None] == bands[None, :]
    keymask = jnp.any(onehot[None] & my_row[:, None, :], axis=-1)
    top = jnp.full((local_heads, q_rows), -1e30, jnp.float32)
    k_heads = k_piece.reshape(count, local_heads, HD)
    v_heads = v_piece.reshape(count, local_heads, HD)
    scores = (
        jnp.einsum("qhd,khd->hqk", q_heads, k_heads, preferred_element_type=jnp.float32) * scale
    )
    scores = jnp.where(keymask[:, None, :], scores, -1e30)
    new_top = jnp.maximum(top, jnp.max(scores, axis=-1))
    expo = jnp.where(keymask[:, None, :], jnp.exp(scores - new_top[..., None]), 0.0)
    total = jnp.sum(expo, axis=-1)
    accum = jnp.einsum(
        "hqk,khd->hqd", expo.astype(jnp.bfloat16), v_heads, preferred_element_type=jnp.float32
    )
    top, total, accum = (new_top, total, accum)
    attn = accum / total[..., None]
    own_rows = jnp.transpose(attn, (1, 0, 2)).reshape(q_rows, local_heads * HD).astype(jnp.bfloat16)
    partner = swapped(own_rows, "cfg", 0)
    first_copy = lax.axis_index("cfg") == 0
    cond = jnp.where(first_copy, own_rows, partner).astype(jnp.float32)
    uncond = jnp.where(first_copy, partner, own_rows).astype(jnp.float32)
    guided = (uncond + guidance[0] * (cond - uncond)).astype(jnp.bfloat16)
    terms = jnp.dot(guided, out_weight, preferred_element_type=jnp.float32)
    return lax.psum_scatter(terms.astype(jnp.bfloat16), "head", scatter_dimension=1, tiled=True)


def shards(queries, *rest):
    seq = lax.axis_size("seq")
    heads = queries.shape[2] // HD
    sets = lax.axis_size("groups")
    pairs = lax.axis_size("cfg") == 2 and lax.axis_size("head") == 2 and sets > 1
    if pairs and heads % seq == 0 and seq % sets == 0 and seq & (seq - 1) == 0:
        return by_heads(queries, *rest)
    return by_rows(queries, *rest)


def solution(mesh):
    in_specs = (
        P("cfg", ("groups", "seq"), "head"),
        P("cfg", ("groups", "seq"), "head"),
        P("cfg", ("groups", "seq"), "head"),
        P(("groups", "head"), None, None),
        P("head", "cfg"),
        P(),
    )
    out_specs = P(("groups", "seq"), ("cfg", "head"))
    return jax.shard_map(shards, mesh=mesh, in_specs=in_specs, out_specs=out_specs, check_vma=False)
```

time: 54.3 us -> 50.4 us (0.928)
  Pallas kernels: 50.3 us -> 47.9 us
  local copies, waits for them, and re-layouts: 3.02 us -> 1.62 us
    pallas_call x1, Pallas kernels: 50.3 us -> 47.9 us  [by_heads(): pl.pallas_call(functools.partial(kernel, n, hp, sets), out_shape=jax.Shap...]
    unnamed x2 -> x1, local copies, waits for them, and re-layouts: 3.02 us -> 1.62 us
where the time goes in v2:
time: 50.4 us; the launch traced here: 50.2 us
  Pallas kernels  47.9 us (95%)
  local copies, waits for them, and re-layouts  1.62 us (3%)
  between operations  0.66 us (1%)
    pallas_call x1, Pallas kernels, by_heads(): pl.pallas_call(functools.partial(kernel, n, hp, sets), out_shape=jax.Shap...  47.9 us
    unnamed x1, local copies, waits for them, and re-layouts  1.62 us

profile of v2, /device:TPU:0, one launch (start us, length us, event | category | flops | bytes accessed | tf_op | source)
XLA Modules:
  0.0 50.2 jit_solution(3769319944641930639)
XLA Ops:
  0.7 47.9 %by_heads.1 = bf16[128,768]{1,0:T(8,128)(2,1)} custom-call(bf16[1,128,1536]{2,1,0:T(8,128)(2,1)} %q_ref.1, bf16[1,128,1536]{2,1,0:T(8,128)(2,1)} %k_ref.1, bf16[1,128,1536]{2,1,0:T(8,128)(2,1)} %v_ref.1, s32[4,4,12]{2,1,0:T(4,128)} %bitcast.1, bf16[1536,1536]{1,0:T(8,128)(2,1)} %w_ref.1, f32[1]{0:T(128)S(6)} %copy.8.g_ref), custom_call_target="tpu_custom_call" | custom-call | tf_op jit(solution)/shard_map/by_heads/pallas_call | solution.py:198
  48.6 1.6 %copy.9 = bf16[128,768]{1,0:T(8,128)(2,1)} copy(bf16[128,768]{1,0:T(8,128)(2,1)} %by_heads.1) | data formatting | bytes 393216

commit v3 on v2

--- a/solution.py
+++ b/solution.py
@@ -45,14 +45,13 @@
     half = T // 2
     cols = out_ref.shape[1]
     share = n // sets
-    tensors = ((q_ref, q_buf), (k_ref, k_buf), (v_ref, v_buf))
+    tensors = ((k_ref, k_buf), (v_ref, v_buf), (q_ref, q_buf))
     sibling = {"cfg": 1 - core}
     across = {"head": 1 - side}
-    facing = {"head": 1 - side, "cfg": 1 - core}
     groups = [{"groups": lax.rem(group + d, sets)} for d in range(1, sets)]
 
     barrier = pltpu.get_barrier_semaphore()
-    for device in [{"seq": flipped(me, k)} for k in range(1, n)] + [sibling, across, facing] + groups:
+    for device in [{"seq": flipped(me, k)} for k in range(1, n)] + [sibling, across] + groups:
         pl.semaphore_signal(barrier, inc=1, device_id=device, device_id_type=MESH)
 
     loads = {}
@@ -71,20 +70,59 @@
             w_loads[j, z] = pltpu.make_async_copy(
                 w_ref.at[pl.ds((z * hp + j) * HD, HD), own_cols], w_buf.at[0, j, pl.ds(z * HD, HD), :], w_sem.at[j, z]
             )
-    pl.semaphore_wait(barrier, n - 1 + 3 + sets - 1)
-
-    a2a = {}
-    across_w = {}
-    their_cols = pl.ds(pl.multiple_of((1 - side) * cols, cols), cols)
-    for j in range(hp):
-        for k in range(n - 1, 0, -1):
-            dest = flipped(me, k)
-            at = pl.multiple_of((dest * hp + j) * HD, HD)
-            for i, (ref, buf) in enumerate(tensors):
+    pl.semaphore_wait(barrier, n - 1 + 2 + sets - 1)
+
+    order = list(range(n - 1, 0, -1))
+    a2a, across_w, swaps, backs, relays, group_w = {}, {}, {}, {}, {}, {}
+    my_half = pl.ds(pl.multiple_of(core * half, half), half)
+    own_at = pl.multiple_of(me * HD, HD)
+
+    def exchange(j):
+        for i, (ref, buf) in enumerate(tensors):
+            for k in order:
+                dest = flipped(me, k)
+                at = pl.multiple_of((dest * hp + j) * HD, HD)
                 a2a[j, k, i] = remote(
                     ref.at[0, :, pl.ds(at, HD)], buf.at[j, pl.ds(mine, T), :],
                     a_send.at[j, k - 1, i], a_recv.at[j, k - 1, i], {"seq": dest},
                 )
+
+    def place(slot, j, k):
+        at = pl.multiple_of(flipped(me, k) * HD, HD)
+        return rows.at[slot, j, my_half, pl.ds(at, HD)]
+
+    def relay(kind, j, k, block, slot, device):
+        relays[j, k, kind] = remote(
+            block, place(slot, j, k), f_send.at[kind, j, k], f_recv.at[kind, j, k], device
+        )
+
+    def pass_on(j):
+        for k in order:
+            backs[j, k].wait_recv()
+            relay(1, j, k, place(0, j, k), 1, across)
+            relay(0, j, k, place(0, j, k), 0, sibling)
+
+    def spread(j):
+        for k in [0] + order:
+            relays[j, k, 1].wait_recv()
+            relay(2, j, k, place(1, j, k), 1, sibling)
+
+    def project(j, slot):
+        for k in range(n):
+            for kind in ((0,), (2,))[slot]:
+                relays[j, k, kind].wait_recv()
+        term = jnp.dot(rows[slot, j], w_buf[slot, j], preferred_element_type=jnp.float32)
+        if j + slot > 0:
+            term = acc[...] + term
+        if slot == 1 and j == hp - 1:
+            out_ref[...] = term.astype(jnp.bfloat16)
+        else:
+            acc[...] = term
+
+    their_cols = pl.ds(pl.multiple_of((1 - side) * cols, cols), cols)
+    for j in range(hp):
+        if j < 2:
+            exchange(j)
         for i in range(share):
             z = group * share + i
             at = pl.multiple_of((z * hp + j) * HD, HD)
@@ -99,13 +137,44 @@
     scale = HD ** (-0.5) * LOG2E
     guidance = g_ref[0]
     first = core == 0
-    my_half = pl.ds(pl.multiple_of(core * half, half), half)
-    swaps, backs, relays, group_w = {}, {}, {}, {}
-
-    def pass_on(j, src, block, z, at):
-        for i, (slot, device) in enumerate(((0, sibling), (1, across), (1, facing))):
-            relays[j, src, i] = remote(
-                block, rows.at[slot, j, my_half, pl.ds(at, HD)], f_send.at[i, j, src], f_recv.at[i, j, src], device
+
+    def attend(j, k):
+        head = me * hp + j
+        t = flipped(me, k)
+        q = q_buf[j, pl.ds(pl.multiple_of(t * T, T), T), :]
+        s = lax.dot_general(q, k_buf[j], (((1,), (1,)), ((), ())), preferred_element_type=jnp.float32)
+        pieces = []
+        for b in range(n):
+            listed = mask_ref[t, b, head] + (t == b).astype(jnp.int32)
+            bias = jnp.where(listed > 0, 0.0, -1e30).astype(jnp.float32)
+            pieces.append(s[:, b * T:(b + 1) * T] * scale + bias)
+        s = jnp.concatenate(pieces, axis=1)
+        top = jnp.max(s, axis=1, keepdims=True)
+        expo = jnp.exp2(s - top)
+        total = jnp.sum(expo, axis=1, keepdims=True)
+        o = jnp.dot(expo.astype(jnp.bfloat16), v_buf[j], preferred_element_type=jnp.float32)
+        o = (o * (1.0 / total)).astype(jnp.bfloat16)
+        att[j, 0, t] = o[:half]
+        att[j, 1, t] = o[half:]
+        swaps[j, k] = remote(att.at[j, 1 - core, t], other.at[j, t], x_send.at[j, k], x_recv.at[j, k], sibling)
+
+    def guide(j, k):
+        t = flipped(me, k)
+        swaps[j, k].wait_recv()
+        own = att[j, core, t].astype(jnp.float32)
+        oth = other[j, t].astype(jnp.float32)
+        cond = jnp.where(first, own, oth)
+        uncond = jnp.where(first, oth, own)
+        guided = (uncond + guidance * (cond - uncond)).astype(jnp.bfloat16)
+        guid[j, t] = guided
+        if k == 0:
+            rows[0, j, my_half, pl.ds(own_at, HD)] = guided
+            relay(1, j, 0, guid.at[j, t], 1, across)
+            relay(0, j, 0, guid.at[j, t], 0, sibling)
+        else:
+            backs[j, k] = remote(
+                guid.at[j, t], rows.at[0, j, my_half, pl.ds(own_at, HD)],
+                r_send.at[j, k - 1], r_recv.at[j, k - 1], {"seq": t},
             )
 
     for j in range(hp):
@@ -117,66 +186,41 @@
                 group_w[d, j, i] = remote(block, block, wy_send.at[d, j, i], wy_recv.at[d, j, i], device)
         for i in range(3):
             loads[j, i].wait()
-            for k in range(1, n):
+        for i in range(2):
+            for k in order:
                 a2a[j, k, i].wait_recv()
-        head = me * hp + j
-        for t in range(n):
-            q = q_buf[j, t * T:(t + 1) * T, :]
-            s = lax.dot_general(q, k_buf[j], (((1,), (1,)), ((), ())), preferred_element_type=jnp.float32)
-            pieces = []
-            for b in range(n):
-                piece = s[:, b * T:(b + 1) * T] * scale
-                if b != t:
-                    piece = piece + jnp.where(mask_ref[t, b, head] > 0, 0.0, -1e30).astype(jnp.float32)
-                pieces.append(piece)
-            s = jnp.concatenate(pieces, axis=1)
-            top = jnp.max(s, axis=1, keepdims=True)
-            expo = jnp.exp2(s - top)
-            total = jnp.sum(expo, axis=1, keepdims=True)
-            o = jnp.dot(expo.astype(jnp.bfloat16), v_buf[j], preferred_element_type=jnp.float32)
-            o = (o * (1.0 / total)).astype(jnp.bfloat16)
-            att[j, 0, t] = o[:half]
-            att[j, 1, t] = o[half:]
-        swaps[j] = remote(att.at[j, 1 - core], other.at[j], x_send.at[j], x_recv.at[j], sibling)
-        swaps[j].wait_recv()
-        own = att[j, core].astype(jnp.float32)
-        oth = other[j].astype(jnp.float32)
-        cond = jnp.where(first, own, oth)
-        uncond = jnp.where(first, oth, own)
-        guid[j] = (uncond + guidance * (cond - uncond)).astype(jnp.bfloat16)
-        own_at = pl.multiple_of(me * HD, HD)
-        for k in range(n - 1, 0, -1):
-            dest = flipped(me, k)
-            backs[j, k] = remote(
-                guid.at[j, dest], rows.at[0, j, my_half, pl.ds(own_at, HD)],
-                r_send.at[j, k - 1], r_recv.at[j, k - 1], {"seq": dest},
-            )
-        pass_on(j, 0, guid.at[j, me], me, own_at)
-        rows[0, j, my_half, pl.ds(own_at, HD)] = guid[j, me]
-
-    for j in range(hp):
-        for k in range(1, n):
-            backs[j, k].wait_recv()
-            z = flipped(me, k)
-            at = pl.multiple_of(z * HD, HD)
-            pass_on(j, k, rows.at[0, j, my_half, pl.ds(at, HD)], z, at)
+        before = None
+        for k in [0] + order:
+            if k > 0:
+                a2a[j, k, 2].wait_recv()
+            attend(j, k)
+            if before is not None:
+                guide(j, before)
+            before = k
+        guide(j, before)
+        if j + 2 < hp:
+            exchange(j + 2)
+        if j > 0:
+            pass_on(j - 1)
+        if j > 1:
+            spread(j - 2)
 
     for copy in w_loads.values():
         copy.wait()
     for copy in group_w.values():
         copy.wait_recv()
-    for j in range(hp):
-        for slot, kinds in ((0, (0,)), (1, (1, 2))):
-            for k in range(n):
-                for i in kinds:
-                    relays[j, k, i].wait_recv()
-            term = jnp.dot(rows[slot, j], w_buf[slot, j], preferred_element_type=jnp.float32)
-            if j + slot > 0:
-                term = acc[...] + term
-            if slot == 1 and j == hp - 1:
-                out_ref[...] = term.astype(jnp.bfloat16)
-            else:
-                acc[...] = term
+    for j in range(hp - 2):
+        project(j, 0)
+        project(j, 1)
+    if hp > 1:
+        spread(hp - 2)
+    pass_on(hp - 1)
+    if hp > 1:
+        project(hp - 2, 0)
+        project(hp - 2, 1)
+    spread(hp - 1)
+    project(hp - 1, 0)
+    project(hp - 1, 1)
     for copies in (a2a, across_w, swaps, backs, relays, group_w):
         for copy in copies.values():
             copy.wait_send()
@@ -212,7 +256,7 @@
             pltpu.VMEM((T, cols), jnp.float32),
             dma((hp, 3)), dma((hp, n)),
             dma((hp, n - 1, 3)), dma((hp, n - 1, 3)),
-            dma((hp,)), dma((hp,)),
+            dma((hp, n)), dma((hp, n)),
             dma((hp, n - 1)), dma((hp, n - 1)),
             dma((3, hp, n)), dma((3, hp, n)),
             dma((hp, share)), dma((hp, share)),

time: 50.4 us -> 50.9 us (level)
  no operation moved by 1% of the time
where the time goes in v3:
time: 50.9 us; the launch traced here: 50.4 us
  Pallas kernels  48.2 us (95%)
  local copies, waits for them, and re-layouts  1.62 us (3%)
  between operations  0.66 us (1%)
    pallas_call x1, Pallas kernels, by_heads(): pl.pallas_call(functools.partial(kernel, n, hp, sets), out_shape=jax.Shap...  48.2 us
    unnamed x1, local copies, waits for them, and re-layouts  1.62 us

profile of v3, /device:TPU:0, one launch (start us, length us, event | category | flops | bytes accessed | tf_op | source)
XLA Modules:
  0.0 50.4 jit_solution(13234199527994496063)
XLA Ops:
  0.7 48.2 %by_heads.1 = bf16[128,768]{1,0:T(8,128)(2,1)} custom-call(bf16[1,128,1536]{2,1,0:T(8,128)(2,1)} %q_ref.1, bf16[1,128,1536]{2,1,0:T(8,128)(2,1)} %k_ref.1, bf16[1,128,1536]{2,1,0:T(8,128)(2,1)} %v_ref.1, s32[4,4,12]{2,1,0:T(4,128)} %bitcast.1, bf16[1536,1536]{1,0:T(8,128)(2,1)} %w_ref.1, f32[1]{0:T(128)S(6)} %copy.8.g_ref), custom_call_target="tpu_custom_call" | custom-call | tf_op jit(solution)/shard_map/by_heads/pallas_call | solution.py:242
  48.8 1.6 %copy.9 = bf16[128,768]{1,0:T(8,128)(2,1)} copy(bf16[128,768]{1,0:T(8,128)(2,1)} %by_heads.1) | data formatting | bytes 393216

commit v4 on v2

--- a/solution.py
+++ b/solution.py
@@ -76,7 +76,7 @@
     a2a = {}
     across_w = {}
     their_cols = pl.ds(pl.multiple_of((1 - side) * cols, cols), cols)
-    for j in range(hp):
+    def exchange(j):
         for k in range(n - 1, 0, -1):
             dest = flipped(me, k)
             at = pl.multiple_of((dest * hp + j) * HD, HD)
@@ -85,6 +85,10 @@
                     ref.at[0, :, pl.ds(at, HD)], buf.at[j, pl.ds(mine, T), :],
                     a_send.at[j, k - 1, i], a_recv.at[j, k - 1, i], {"seq": dest},
                 )
+
+    for j in range(hp):
+        if j < 2:
+            exchange(j)
         for i in range(share):
             z = group * share + i
             at = pl.multiple_of((z * hp + j) * HD, HD)
@@ -107,6 +111,13 @@
             relays[j, src, i] = remote(
                 block, rows.at[slot, j, my_half, pl.ds(at, HD)], f_send.at[i, j, src], f_recv.at[i, j, src], device
             )
+
+    def forward(j):
+        for k in range(1, n):
+            backs[j, k].wait_recv()
+            z = flipped(me, k)
+            at = pl.multiple_of(z * HD, HD)
+            pass_on(j, k, rows.at[0, j, my_half, pl.ds(at, HD)], z, at)
 
     for j in range(hp):
         for i in range(share):
@@ -153,13 +164,13 @@
             )
         pass_on(j, 0, guid.at[j, me], me, own_at)
         rows[0, j, my_half, pl.ds(own_at, HD)] = guid[j, me]
-
-    for j in range(hp):
-        for k in range(1, n):
-            backs[j, k].wait_recv()
-            z = flipped(me, k)
-            at = pl.multiple_of(z * HD, HD)
-            pass_on(j, k, rows.at[0, j, my_half, pl.ds(at, HD)], z, at)
+        if j + 2 < hp:
+            exchange(j + 2)
+        if 0 < j < hp - 1:
+            forward(j - 1)
+
+    for j in range(max(hp - 2, 0), hp):
+        forward(j)
 
     for copy in w_loads.values():
         copy.wait()

time: 50.4 us -> 49.3 us (0.978)
  Pallas kernels: 47.9 us -> 46.9 us
    pallas_call x1, Pallas kernels: 47.9 us -> 46.9 us  [by_heads(): pl.pallas_call(functools.partial(kernel, n, hp, sets), out_shape=jax.Shap...]
where the time goes in v4:
time: 49.3 us; the launch traced here: 49.1 us
  Pallas kernels  46.9 us (95%)
  local copies, waits for them, and re-layouts  1.62 us (3%)
  between operations  0.66 us (1%)
    pallas_call x1, Pallas kernels, by_heads(): pl.pallas_call(functools.partial(kernel, n, hp, sets), out_shape=jax.Shap...  46.9 us
    unnamed x1, local copies, waits for them, and re-layouts  1.62 us

profile of v4, /device:TPU:0, one launch (start us, length us, event | category | flops | bytes accessed | tf_op | source)
XLA Modules:
  0.0 49.1 jit_solution(12290635275314364904)
XLA Ops:
  0.7 46.9 %by_heads.1 = bf16[128,768]{1,0:T(8,128)(2,1)} custom-call(bf16[1,128,1536]{2,1,0:T(8,128)(2,1)} %q_ref.1, bf16[1,128,1536]{2,1,0:T(8,128)(2,1)} %k_ref.1, bf16[1,128,1536]{2,1,0:T(8,128)(2,1)} %v_ref.1, s32[4,4,12]{2,1,0:T(4,128)} %bitcast.1, bf16[1536,1536]{1,0:T(8,128)(2,1)} %w_ref.1, f32[1]{0:T(128)S(6)} %copy.8.g_ref), custom_call_target="tpu_custom_call" | custom-call | tf_op jit(solution)/shard_map/by_heads/pallas_call | solution.py:209
  47.5 1.6 %copy.9 = bf16[128,768]{1,0:T(8,128)(2,1)} copy(bf16[128,768]{1,0:T(8,128)(2,1)} %by_heads.1) | data formatting | bytes 393216
